TPU v7x, 256 devices: a whole 4x4x8 slice. The times are simulated.
256 devices in a mesh: req: 32 (over y, x, z_hi), tp: 8 (over z_lo, core).
Axes of the slice: x: 4, y: 4, z: 8 (z_hi: 2, z_lo: 4; z = z_hi * 4 + z_lo), core: 2. Of those that a mesh axis runs over, the one named last changes fastest.
Arguments:
- residual: bfloat16 [8192, 2304], P('req'), may hold values from -58 to 58
- context: bfloat16 [8192, 2304], P('req', 'tp'), may hold values from -6 to 6
- attention_output_weight: bfloat16 [2304, 2304], P('tp'), may hold values from -0.1875 to 0.1875
- adapter_down_maps: bfloat16 [64, 2304, 16], P('req', 'tp'), may hold values from -0.125 to 0.125
- adapter_up_maps: bfloat16 [64, 16, 2304], P('req'), may hold values from -1.5 to 1.5
- adapter_storage_row: int32 [64], replicated, may hold values from 0 to 63, each once
- active_adapters: int32 [16], replicated, may hold values from 0 to 63, as said below
- request_token_length: int32 [32, 4], P('req'), may hold values from 1 to 128, 256 in all within a row
- request_adapter_entry: int32 [32, 4], P('req'), may hold values from 0 to 15
- expert_norm_gain: bfloat16 [2304], replicated, may hold values from 0.099609375 to 1.8984375
- router_projection: bfloat16 [2304, 8], replicated, may hold values from -0.125 to 0.125
- expert_choice_pairs: int32 [8192, 2], P('req'), may hold values from 0 to 7, all different within a row; in each aligned block of 256 rows (0 to 255, 256 to 511, ...) at most 80 rows name the same one
- expert_gate_weight: bfloat16 [32, 2304, 5760], P('req', None, 'tp'), as said below
- expert_up_weight: bfloat16 [32, 2304, 5760], P('req', None, 'tp'), as said below
- expert_down_weight: bfloat16 [32, 5760, 2304], P('req', 'tp'), as said below
Outputs:
- layer_out: bfloat16 [8192, 2304], P('req', 'tp')
Inputs may be any that keep to these rules, and one draw needn't show every extreme that they name: `active_adapters`: 16 different adapter numbers, 0 and 63 among them. `adapter_storage_row`: every stored row appears once. `request_token_length`: each group's lengths sum to 256; the longest request of a group has exactly half of 256 tokens. `expert_choice_pairs`: each row names two different experts; within the 256 rows of one group no expert is named by more than 80 rows, a bound that some block reaches. `expert_gate_weight`: the 4 holders c * 8 + e of expert e hold the same weights. `expert_up_weight`: the 4 holders c * 8 + e of expert e hold the same weights. `expert_down_weight`: the 4 holders c * 8 + e of expert e hold the same weights.
All inputs are finite; a program needn't handle non-finite values.
Results may differ from a plain program's by a relative error of at most 0.0095.
Values may be sent and summed in bfloat16 or wider, within the bound.
A program may use at most 128 MiB of HBM per device.

v0:
```python
import jax
import jax.numpy as jnp
from jax import lax
from jax.sharding import Mesh
from jax.sharding import PartitionSpec as P

CAP = 80
NORM_EPS = 1e-05
REQ = ("ry", "rxz")


def segment_onehot(request_token_length, token_count):
    bounds = jnp.cumsum(request_token_length[0])
    position = jnp.arange(token_count, dtype=jnp.int32)
    segment = jnp.sum((position[:, None] >= bounds[None, :]).astype(jnp.int32), axis=1)
    slot_range = jnp.arange(request_token_length.shape[1], dtype=jnp.int32)
    return segment[:, None] == slot_range[None, :]


def route_tables(expert_choice_pairs, expert_count, capacity):
    expert_ids = jnp.arange(expert_count, dtype=jnp.int32)
    first_hit = expert_choice_pairs[None, :, 0] == expert_ids[:, None]
    second_hit = expert_choice_pairs[None, :, 1] == expert_ids[:, None]
    chosen = first_hit | second_hit
    slot_of = jnp.cumsum(chosen.astype(jnp.int32), axis=1) - 1
    slot_range = jnp.arange(capacity, dtype=jnp.int32)
    placement = chosen[:, None, :] & (slot_of[:, None, :] == slot_range[None, :, None])
    return (placement, first_hit, second_hit)


def on_device(
    residual,
    context,
    attention_output_weight,
    adapter_down_maps,
    adapter_up_maps,
    adapter_storage_row,
    active_adapters,
    request_token_length,
    request_adapter_entry,
    expert_norm_gain,
    router_projection,
    expert_choice_pairs,
    expert_gate_weight,
    expert_up_weight,
    expert_down_weight,
):
    token_count = residual.shape[0]
    hidden_width = residual.shape[1]
    feature_share = context.shape[1]
    local_rows = adapter_down_maps.shape[0]
    adapter_rank_size = adapter_down_maps.shape[2]
    request_count = request_token_length.shape[1]
    share_width = hidden_width // lax.axis_size("tp")
    share_start = lax.axis_index("tp") * share_width
    up_slice = lax.dynamic_slice_in_dim(adapter_up_maps, share_start, share_width, 2)
    packed = jnp.concatenate(
        [
            adapter_down_maps.reshape(local_rows, feature_share * adapter_rank_size),
            up_slice.reshape(local_rows, adapter_rank_size * share_width),
        ],
        axis=1,
    )
    all_packed = lax.all_gather(packed, REQ, axis=0, tiled=True)
    request_rows = adapter_storage_row[active_adapters[request_adapter_entry[0]]]
    picked = all_packed[request_rows]
    down_req = picked[:, : feature_share * adapter_rank_size].reshape(
        request_count, feature_share, adapter_rank_size
    )
    up_req = picked[:, feature_share * adapter_rank_size :].reshape(
        request_count * adapter_rank_size, share_width
    )
    down_joined = jnp.transpose(down_req, (1, 0, 2)).reshape(
        feature_share, request_count * adapter_rank_size
    )
    segment_hot = segment_onehot(request_token_length, token_count)
    low_all = jnp.dot(context, down_joined, preferred_element_type=jnp.float32)
    reduced_mask = jnp.repeat(segment_hot, adapter_rank_size, axis=1)
    low_part = jnp.where(reduced_mask, low_all, 0.0)
    low_total = lax.psum(low_part, "tp").astype(jnp.bfloat16)
    lora_share = jnp.dot(low_total, up_req, preferred_element_type=jnp.float32)
    base = jnp.dot(context, attention_output_weight, preferred_element_type=jnp.float32)
    base_share = lax.dynamic_slice_in_dim(base, share_start, share_width, 1)
    head_part = lax.dynamic_update_slice_in_dim(base, base_share + lora_share, share_start, 1)
    gain_all = expert_norm_gain.astype(jnp.float32)
    head_sum = lax.psum(head_part.astype(jnp.bfloat16), "tp").astype(jnp.float32)
    blended_rows = residual.astype(jnp.float32) + head_sum
    mean_square = jnp.mean(blended_rows * blended_rows, axis=1, keepdims=True)
    normed = (blended_rows * lax.rsqrt(mean_square + NORM_EPS) * gain_all).astype(jnp.bfloat16)
    mixed_share = lax.dynamic_slice_in_dim(blended_rows, share_start, share_width, 1)
    logits = jnp.dot(normed, router_projection, preferred_element_type=jnp.float32)
    expert_count = router_projection.shape[1]
    expert_range = jnp.arange(expert_count, dtype=jnp.int32)
    logit_first = jnp.sum(
        jnp.where(expert_choice_pairs[:, 0:1] == expert_range[None, :], logits, 0.0), axis=1
    )
    logit_second = jnp.sum(
        jnp.where(expert_choice_pairs[:, 1:2] == expert_range[None, :], logits, 0.0), axis=1
    )
    weight_first = 1.0 / (1.0 + jnp.exp(logit_second - logit_first))
    weight_second = 1.0 / (1.0 + jnp.exp(logit_first - logit_second))
    placement, first_hit, second_hit = route_tables(expert_choice_pairs, expert_count, CAP)
    send_rows = jnp.einsum(
        "est,td->esd", placement.astype(jnp.bfloat16), normed, preferred_element_type=jnp.float32
    ).astype(jnp.bfloat16)
    rows_in = lax.all_to_all(send_rows, "rxz", split_axis=0, concat_axis=0, tiled=True)
    rows_flat = rows_in.reshape(expert_count * CAP, hidden_width)
    gate_value = jnp.dot(rows_flat, expert_gate_weight[0], preferred_element_type=jnp.float32)
    up_value = jnp.dot(rows_flat, expert_up_weight[0], preferred_element_type=jnp.float32)
    hidden = (jax.nn.silu(gate_value) * up_value).astype(jnp.bfloat16)
    partial_value = jnp.dot(hidden, expert_down_weight[0], preferred_element_type=jnp.float32)
    returned = lax.all_to_all(
        partial_value.astype(jnp.bfloat16).reshape(expert_count, CAP, hidden_width),
        "rxz",
        split_axis=0,
        concat_axis=0,
        tiled=True,
    )
    token_weight = jnp.where(first_hit, weight_first[None, :], 0.0) + jnp.where(
        second_hit, weight_second[None, :], 0.0
    )
    scaled_place = placement.astype(jnp.float32) * token_weight[:, None, :]
    contribution = jnp.einsum(
        "est,esd->td",
        scaled_place,
        returned.astype(jnp.float32),
        precision=lax.Precision.HIGHEST,
        preferred_element_type=jnp.float32,
    )
    moe_share = lax.psum_scatter(
        contribution.astype(jnp.bfloat16), "tp", scatter_dimension=1, tiled=True
    ).astype(jnp.float32)
    return (mixed_share + moe_share).astype(jnp.bfloat16)


def solution(mesh):
    req_size = mesh.shape["req"]
    plane = 8
    split_mesh = Mesh(
        mesh.devices.reshape(req_size // plane, plane, mesh.shape["tp"]), ("ry", "rxz", "tp")
    )
    return jax.shard_map(
        on_device,
        mesh=split_mesh,
        in_specs=(
            P(REQ, None),
            P(REQ, "tp"),
            P("tp", None),
            P(REQ, "tp", None),
            P(REQ, None, None),
            P(),
            P(),
            P(REQ, None),
            P(REQ, None),
            P(),
            P(),
            P(REQ, None),
            P(REQ, None, "tp"),
            P(REQ, None, "tp"),
            P(REQ, "tp", None),
        ),
        out_specs=P(REQ, "tp"),
        check_vma=False,
    )
```

profile of v0, /device:TPU:4, one launch (start us, length us, event | category | flops | bytes accessed | tf_op | source)
XLA Modules:
  0.0 434.4 jit_solution(16234100951384589022)
XLA Ops:
  6.5 0.0 copy-start
  6.5 0.0 all-gather.3.cloned.1.call-start
  6.5 1.0 constant_dynamic-slice_fusion
  7.5 0.1 reshape.268
  7.6 0.9 copy.29
  8.5 0.2 reshape.267
  8.7 0.7 maximum_bitcast_fusion
  9.3 0.0 all-gather.3.cloned.1.call-update
  9.4 0.0 all-reduce.2.cloned.1.call-start
  9.4 0.8 reduce-window.18
  10.2 0.7 fusion.27
  10.9 1.3 gather_fusion
  12.2 1.3 gather_fusion.1
  13.5 0.1 convert_reduce_fusion
  13.6 3.6 fusion.35
  17.2 0.0 copy-start.4
  17.2 77.7 %all-gather.3.cloned.1.call-done = bf16[32,2,9216]{2,1,0:T(2,128)(2,1)} async-done(((bf16[1,2,9216]{2,1,0:T(2,128)(2,1)}), bf16[32,2,9216]{2,1,0:T(2,128)(2,1)}) %all-gather.3.cloned.1.call-update) | async-done | bytes 1179664 | tf_op jit(solution)/shard_map/all_gather | solution.py:64
  94.9 2.3 reshape.300
  97.3 2.1 gather_fusion.2
  99.4 0.6 fusion.33
  100.0 1.5 reshape.271
  101.5 1.7 reshape.269
  103.3 1.7 copy.30
  105.0 0.0 copy-done.4
  105.0 1.0 fusion.10
  106.0 26.3 %psum.14 = bf16[256,64]{0,1:T(8,128)(2,1)S(1)} all-reduce(f32[256,64]{0,1:T(8,128)S(1)} %fusion.10), channel_id=1, replica_groups=mesh['ry'=4,'rxz'=8,'tp'=8] {'tp'}, use_global_device_ids=true, to_apply=%region_2.3 | all-reduce | flops 16384 | bytes 98304 | tf_op jit(solution)/shard_map/psum | solution.py:80
  132.3 2.1 convolution_add_fusion
  134.4 3.5 dynamic_update_slice.3
  137.9 0.0 copy-start.6
  137.9 0.0 copy-start.5
  137.9 2.8 convert_element_type.49
  140.7 0.0 all-reduce.2.cloned.1.call-update
  140.7 0.0 copy-done.6
  140.8 0.6 reduce-window.19
  141.3 0.2 slice_reduce_fusion
  141.6 0.0 copy-done.5
  141.6 0.1 add_bitcast_fusion
  141.7 69.1 %all-reduce.2.cloned.1.call-done = bf16[256,2304]{1,0:T(8,128)(2,1)} async-done(((bf16[256,2304]{1,0:T(8,128)(2,1)}), bf16[256,2304]{1,0:T(8,128)(2,1)}) %all-reduce.2.cloned.1.call-update) | async-done | bytes 1179664 | tf_op jit(solution)/shard_map/psum | solution.py:86
  210.8 0.0 copy-start.1
  210.8 0.0 copy-start.2
  210.8 3.6 convert_add_fusion
  214.4 0.0 copy-done.1
  214.4 0.0 copy-done.2
  214.4 1.2 convolution_convert_fusion.1
  215.6 0.0 copy-start.7
  215.6 74.4 %all_to_all.10 = bf16[8,80,2304]{2,1,0:T(8,128)(2,1)S(1)} all-to-all(bf16[8,80,2304]{2,1,0:T(8,128)(2,1)S(1)} %convolution_convert_fusion.1), channel_id=1, replica_groups=mesh['ry'=4,'rxz'=8,'tp'=8] {'rxz'}, dimensions={0} | all-to-all | bytes 5898240 | tf_op jit(solution)/shard_map/all_to_all | solution.py:106
  290.0 0.0 copy-start.3
  290.0 1.6 copy-done.3
  291.7 0.0 copy-done.7
  291.7 4.0 fusion.5
  295.6 0.0 copy-done
  295.6 14.5 %convolution_convert_fusion = bf16[640,2304]{1,0:T(8,128)(2,1)} fusion(bf16[1,720,2304]{2,1,0:T(8,128)(2,1)S(1)} %copy-done, f32[640,720]{0,1:T(8,128)} %fusion.5, bf16[640,2304]{1,0:T(8,128)(2,1)} %bitcast.68, bf16[1,2304,720]{1,2,0:T(8,128)(2,1)} %param.28), kind=kOutput, calls=%fused_computation.3 | convolution fusion | flops 4250972160 | bytes 14376960 | tf_op jit(solution)/shard_map/dot_general | solution.py:111
  310.1 0.0 copy-start.8
  310.2 7.4 %all-to-all-start.1 = ((bf16[8,80,2304]{2,1,0:T(8,128)(2,1)}), bf16[8,80,2304]{2,1,0:T(8,128)(2,1)}, u32[]{:S(2)}, u32[]{:S(2)}) async-start(bf16[8,80,2304]{2,1,0:T(8,128)(2,1)} %bitcast.66), calls=%async_computation.1 | async-start | bytes 5898240 | tf_op jit(solution)/shard_map/all_to_all | solution.py:112
  317.5 0.0 reduce-scatter.4.cloned.1.call-start
  317.5 0.0 copy-done.8
  317.5 2.2 select_reduce_fusion.1
  319.8 57.1 %all-to-all-done.1 = bf16[8,80,2304]{2,1,0:T(8,128)(2,1)} async-done(((bf16[8,80,2304]{2,1,0:T(8,128)(2,1)}), bf16[8,80,2304]{2,1,0:T(8,128)(2,1)}, u32[]{:S(2)}, u32[]{:S(2)}) %all-to-all-start.1) | async-done | bytes 2949152 | tf_op jit(solution)/shard_map/all_to_all | solution.py:112
  376.9 6.4 %fusion.1 = bf16[2304,256]{1,0:T(8,128)(2,1)} fusion(bf16[8,80,2304]{2,1,0:T(8,128)(2,1)} %all-to-all-done.1, f32[8,256]{1,0:T(8,128)S(1)} %select_add_fusion, s32[8,256]{1,0:T(8,128)S(1)} %add_bitcast_fusion, pred[8,256]{1,0:T(8,128)(4,1)S(1)} %fusion.24), kind=kOutput, calls=%fused_computation.7 | convolution fusion | flops 4530929664 | bytes 4147200 | tf_op jit(solution)/shard_map/est,esd->td/dot_general | solution.py:123
  383.3 0.0 reduce-scatter.4.cloned.1.call-update
  383.3 39.9 %reduce-scatter.4.cloned.1.call-done = bf16[288,256]{1,0:T(8,128)(2,1)} async-done(((bf16[2304,256]{1,0:T(8,128)(2,1)}), bf16[288,256]{1,0:T(8,128)(2,1)}) %reduce-scatter.4.cloned.1.call-update) | async-done | bytes 147472
  423.2 1.1 copy.36
  424.3 1.9 add_convert_fusion
  426.2 1.7 copy.33
  (16 shorter events, 0.1 us)
Async XLA Ops:
  6.5 289.1 %copy-start = (bf16[1,720,2304]{2,1,0:T(8,128)(2,1)S(1)}, bf16[1,720,2304]{2,1,0:T(8,128)(2,1)}, u32[]{:S(2)}) copy-start(bf16[1,720,2304]{2,1,0:T(8,128)(2,1)} %param.29) | copy-start | bytes 9953284
  6.5 88.4 %all-gather.3.cloned.1.call-start = ((), (), s32[]{:S(2)}) async-start(), calls=%async_computation.4 | async-start | bytes 1216512 | tf_op jit(solution)/shard_map/all_gather | solution.py:64
  9.4 201.5 %all-reduce.2.cloned.1.call-start = ((), (), s32[]{:S(2)}) async-start(), calls=%async_computation.3 | async-start | bytes 2359296 | tf_op jit(solution)/shard_map/psum | solution.py:86
  17.2 87.8 %copy-start.4 = (bf16[256,288]{0,1:T(8,128)(2,1)S(1)}, bf16[256,288]{0,1:T(8,128)(2,1)}, u32[]{:S(2)}) copy-start(bf16[256,288]{0,1:T(8,128)(2,1)} %param.16) | copy-start | bytes 442372
  137.9 2.8 copy-start.6
  137.9 3.7 copy-start.5
  210.8 3.6 copy-start.1
  210.8 3.6 copy-start.2
  215.6 76.1 %copy-start.7 = (bf16[1,2304,720]{1,2,0:T(8,128)(2,1)S(1)}, bf16[1,2304,720]{1,2,0:T(8,128)(2,1)}, u32[]{:S(2)}) copy-start(bf16[1,2304,720]{1,2,0:T(8,128)(2,1)} %param.27) | copy-start | bytes 9953284
  290.0 1.6 copy-start.3
  310.1 7.4 %copy-start.8 = (bf16[2304,8]{0,1:T(8,128)(2,1)S(1)}, bf16[2304,8]{0,1:T(8,128)(2,1)}, u32[]{:S(2)}) copy-start(bf16[2304,8]{0,1:T(8,128)(2,1)} %param.25) | copy-start | bytes 110596
  310.2 66.7 %all-to-all-start.1 = ((bf16[8,80,2304]{2,1,0:T(8,128)(2,1)}), bf16[8,80,2304]{2,1,0:T(8,128)(2,1)}, u32[]{:S(2)}, u32[]{:S(2)}) async-start(bf16[8,80,2304]{2,1,0:T(8,128)(2,1)} %bitcast.66), calls=%async_computation.1 | async-start | bytes 5898240 | tf_op jit(solution)/shard_map/all_to_all | solution.py:112
  317.5 105.7 %reduce-scatter.4.cloned.1.call-start = ((), (), s32[]{:S(2)}) async-start(), calls=%async_computation.5 | async-start | bytes 1327104
Sparse Core Ops, SparseCore 0:
  10.8 84.0 all-gather.2
  140.8 69.9 all-reduce.1
  383.4 39.7 reduce-scatter.3
where the time goes:
time: 435 us; the launch traced here: 434 us
  waiting for transfers between devices  244 us (56%)
  blocking collectives  101 us (23%)
  matrix products  34.9 us (8%)
  local copies, waits for them, and re-layouts  22.9 us (5%)
  between operations  13.2 us (3%)
  other arithmetic  11.3 us (3%)
  starting transfers between devices  7.41 us (2%)
    all_gather x1, waiting for transfers between devices, on_device(): all_packed = lax.all_gather(packed, REQ, axis=0, tiled=True)  77.7 us
    all_to_all x1, blocking collectives, on_device(): lax.all_to_all(send_rows, 'rxz', split_axis=0, concat_axis=0, tiled=True)  74.4 us
    psum x1, waiting for transfers between devices, on_device(): lax.psum(head_part.astype(jnp.bfloat16), 'tp').astype(jnp.float32)  69.1 us
    all_to_all x1, waiting for transfers between devices, on_device(): lax.all_to_all(partial_value.astype(jnp.bfloat16).reshape(expert_count, C...  57.1 us
    unnamed x4, waiting for transfers between devices  40 us
    psum x1, blocking collectives, on_device(): low_total = lax.psum(low_part, 'tp').astype(jnp.bfloat16)  26.3 us
    dot_general x1, matrix products, on_device(): jnp.dot(hidden, expert_down_weight[0], preferred_element_type=jnp.float32)  14.5 us
  transfers between devices with their start and end apart: 4, of which 4 were waited for; matrix products, arithmetic and copies ran while one was open for 3% of the time, Pallas kernels for 0%

commit v1 on v0

--- a/solution.py
+++ b/solution.py
@@ -83,7 +83,9 @@
     base_share = lax.dynamic_slice_in_dim(base, share_start, share_width, 1)
     head_part = lax.dynamic_update_slice_in_dim(base, base_share + lora_share, share_start, 1)
     gain_all = expert_norm_gain.astype(jnp.float32)
-    head_sum = lax.psum(head_part.astype(jnp.bfloat16), "tp").astype(jnp.float32)
+    head_sum = jnp.sum(lax.all_gather(head_part.astype(jnp.bfloat16), "tp"), axis=0).astype(
+        jnp.float32
+    )
     blended_rows = residual.astype(jnp.float32) + head_sum
     mean_square = jnp.mean(blended_rows * blended_rows, axis=1, keepdims=True)
     normed = (blended_rows * lax.rsqrt(mean_square + NORM_EPS) * gain_all).astype(jnp.bfloat16)

time: 435 us -> 469 us (1.078)
  waiting for transfers between devices: 244 us -> 272 us
  other arithmetic: 11.3 us -> 17.5 us
    all_gather x0 -> x1, waiting for transfers between devices: none -> 95.7 us  [on_device(): lax.all_gather(head_part.astype(jnp.bfloat16), 'tp')]
    psum x1 -> x0, waiting for transfers between devices: 69.1 us -> none  [on_device(): lax.psum(head_part.astype(jnp.bfloat16), 'tp').astype(jnp.float32)]
    reduce_scatter x0 -> x1, waiting for transfers between devices: none -> 68.3 us  [on_device(): lax.psum_scatter(contribution.astype(jnp.bfloat16), 'tp', scatter_dimensi...]
    unnamed x4 -> x3, waiting for transfers between devices: 40 us -> 0.05 us
    all_to_all x1, waiting for transfers between devices: 57.1 us -> 30.2 us  [on_device(): lax.all_to_all(partial_value.astype(jnp.bfloat16).reshape(expert_count, C...]
    reduce_sum x0 -> x1, other arithmetic: none -> 6.39 us  [on_device(): jnp.sum(lax.all_gather(head_part.astype(jnp.bfloat16), 'tp'), axis=0)]
where the time goes in v1:
time: 469 us; the launch traced here: 468 us
  waiting for transfers between devices  272 us (58%)
  blocking collectives  101 us (22%)
  matrix products  35 us (7%)
  local copies, waits for them, and re-layouts  24.3 us (5%)
  other arithmetic  17.5 us (4%)
  between operations  13.2 us (3%)
  starting transfers between devices  5.79 us (1%)
    all_gather x1, waiting for transfers between devices, on_device(): lax.all_gather(head_part.astype(jnp.bfloat16), 'tp')  95.7 us
    all_gather x1, waiting for transfers between devices, on_device(): all_packed = lax.all_gather(packed, REQ, axis=0, tiled=True)  77.7 us
    all_to_all x1, blocking collectives, on_device(): lax.all_to_all(send_rows, 'rxz', split_axis=0, concat_axis=0, tiled=True)  74.2 us
    reduce_scatter x1, waiting for transfers between devices, on_device(): lax.psum_scatter(contribution.astype(jnp.bfloat16), 'tp', scatter_dimensi...  68.3 us
    all_to_all x1, waiting for transfers between devices, on_device(): lax.all_to_all(partial_value.astype(jnp.bfloat16).reshape(expert_count, C...  30.2 us
    psum x1, blocking collectives, on_device(): low_total = lax.psum(low_part, 'tp').astype(jnp.bfloat16)  26.3 us
    dot_general x1, matrix products, on_device(): jnp.dot(hidden, expert_down_weight[0], preferred_element_type=jnp.float32)  14.5 us
  transfers between devices with their start and end apart: 4, of which 4 were waited for; matrix products, arithmetic and copies ran while one was open for 3% of the time, Pallas kernels for 0%

profile of v1, /device:TPU:4, one launch (start us, length us, event | category | flops | bytes accessed | tf_op | source)
XLA Modules:
  0.0 468.2 jit_solution(10297106777084233211)
XLA Ops:
  6.5 0.0 copy-start
  6.5 0.0 all-gather.7.cloned.1.call-start
  6.5 1.0 constant_dynamic-slice_fusion
  7.5 0.1 reshape.268
  7.6 0.9 copy.31
  8.5 0.2 reshape.267
  8.7 0.7 maximum_bitcast_fusion
  9.3 0.0 all-gather.7.cloned.1.call-update
  9.4 0.0 all-gather.5.cloned.1.call-start
  9.4 0.8 reduce-window.18
  10.2 0.7 fusion.26
  10.9 1.3 gather_fusion
  12.2 1.3 gather_fusion.1
  13.5 0.1 convert_reduce_fusion
  13.6 3.6 fusion.34
  17.2 77.7 %all-gather.7.cloned.1.call-done = bf16[32,2,9216]{2,1,0:T(2,128)(2,1)} async-done(((bf16[1,2,9216]{2,1,0:T(2,128)(2,1)}), bf16[32,2,9216]{2,1,0:T(2,128)(2,1)}) %all-gather.7.cloned.1.call-update) | async-done | bytes 1179664 | tf_op jit(solution)/shard_map/all_gather | solution.py:64
  94.9 2.3 reshape.301
  97.3 2.1 gather_fusion.2
  99.4 0.6 fusion.32
  100.0 1.7 reshape.269
  101.8 1.7 copy.32
  103.5 0.0 copy-done.4
  103.5 1.0 fusion.9
  104.5 26.3 %psum.7 = bf16[256,64]{0,1:T(8,128)(2,1)S(1)} all-reduce(f32[256,64]{0,1:T(8,128)S(1)} %fusion.9), channel_id=1, replica_groups=mesh['ry'=4,'rxz'=8,'tp'=8] {'tp'}, use_global_device_ids=true, to_apply=%region_2.3 | all-reduce | flops 16384 | bytes 98304 | tf_op jit(solution)/shard_map/psum | solution.py:80
  130.8 0.9 reshape.271
  131.7 2.0 convolution_add_fusion
  133.7 3.5 dynamic_update_slice.3
  137.3 2.8 convert_element_type.51
  140.1 0.0 copy-start.5
  140.1 0.0 copy-start.6
  140.1 0.0 all-gather.5.cloned.1.call-update
  140.1 2.4 copy.30
  142.5 0.0 copy-done.5
  142.5 0.0 copy-done.6
  142.5 0.6 reduce-window.19
  143.1 0.2 slice_reduce_fusion
  143.4 0.1 add_bitcast_fusion
  143.4 95.7 %all-gather.5.cloned.1.call-done = bf16[2048,2304]{1,0:T(8,128)(2,1)} async-done(((bf16[256,2304]{1,0:T(8,128)(2,1)}), bf16[2048,2304]{1,0:T(8,128)(2,1)}) %all-gather.5.cloned.1.call-update) | async-done | bytes 9437200 | tf_op jit(solution)/shard_map/all_gather | solution.py:86
  239.1 6.4 %reduce_sum.49 = bf16[256,2304]{1,0:T(8,128)(2,1)} reduce(bf16[8,256,2304]{2,1,0:T(8,128)(2,1)} %bitcast.62, bf16[]{:T(256)} %constant.33.clone.1), dimensions={0}, to_apply=%region_3.4 | reduce | flops 4128768 | bytes 10616834 | tf_op jit(solution)/shard_map/reduce_sum | solution.py:86
  245.5 2.4 copy.34
  247.9 0.0 copy-start.1
  247.9 0.0 copy-start.2
  247.9 3.6 convert_add_fusion
  251.5 0.0 copy-done.1
  251.5 0.0 copy-done.2
  251.5 1.2 convolution_convert_fusion.1
  252.6 0.0 copy-start.7
  252.7 74.2 %all_to_all.10 = bf16[8,80,2304]{2,1,0:T(8,128)(2,1)S(1)} all-to-all(bf16[8,80,2304]{2,1,0:T(8,128)(2,1)S(1)} %convolution_convert_fusion.1), channel_id=1, replica_groups=mesh['ry'=4,'rxz'=8,'tp'=8] {'rxz'}, dimensions={0} | all-to-all | bytes 5898240 | tf_op jit(solution)/shard_map/all_to_all | solution.py:108
  326.9 0.0 copy-start.3
  326.9 1.6 copy-done.3
  328.5 0.0 copy-done.7
  328.5 4.1 fusion.4
  332.6 0.0 copy-done
  332.6 14.5 %convolution_convert_fusion = bf16[640,2304]{1,0:T(8,128)(2,1)} fusion(bf16[1,720,2304]{2,1,0:T(8,128)(2,1)S(1)} %copy-done, f32[640,720]{0,1:T(8,128)} %fusion.4, bf16[640,2304]{1,0:T(8,128)(2,1)} %bitcast.65, bf16[1,2304,720]{1,2,0:T(8,128)(2,1)} %param.28), kind=kOutput, calls=%fused_computation.3 | convolution fusion | flops 4250972160 | bytes 14376960 | tf_op jit(solution)/shard_map/dot_general | solution.py:113
  347.1 0.0 copy-start.8
  347.1 5.7 %all-to-all-start.1 = ((bf16[8,80,2304]{2,1,0:T(8,128)(2,1)}), bf16[8,80,2304]{2,1,0:T(8,128)(2,1)}, u32[]{:S(2)}, u32[]{:S(2)}) async-start(bf16[8,80,2304]{2,1,0:T(8,128)(2,1)} %bitcast.63), calls=%async_computation.1 | async-start | bytes 5898240 | tf_op jit(solution)/shard_map/all_to_all | solution.py:114
  352.8 0.0 reduce-scatter.2.cloned.1.call-start
  352.8 0.0 copy-done.8
  352.8 2.2 select_reduce_fusion.1
  355.1 30.2 %all-to-all-done.1 = bf16[8,80,2304]{2,1,0:T(8,128)(2,1)} async-done(((bf16[8,80,2304]{2,1,0:T(8,128)(2,1)}), bf16[8,80,2304]{2,1,0:T(8,128)(2,1)}, u32[]{:S(2)}, u32[]{:S(2)}) %all-to-all-start.1) | async-done | bytes 2949152 | tf_op jit(solution)/shard_map/all_to_all | solution.py:114
  385.2 6.4 %fusion = bf16[256,2304]{0,1:T(8,128)(2,1)} fusion(bf16[8,80,2304]{2,1,0:T(8,128)(2,1)} %all-to-all-done.1, f32[8,256]{1,0:T(8,128)S(1)} %select_add_fusion, s32[8,256]{1,0:T(8,128)S(1)} %add_bitcast_fusion, pred[8,256]{1,0:T(8,128)(4,1)S(1)} %fusion.23), kind=kOutput, calls=%fused_computation.6 | convolution fusion | flops 4530929664 | bytes 4147200 | tf_op jit(solution)/shard_map/est,esd->td/dot_general | solution.py:125
  391.6 0.0 reduce-scatter.2.cloned.1.call-update
  391.7 68.3 %reduce-scatter.2.cloned.1.call-done = bf16[256,288]{0,1:T(8,128)(2,1)} async-done(((bf16[256,2304]{0,1:T(8,128)(2,1)}), bf16[256,288]{0,1:T(8,128)(2,1)}) %reduce-scatter.2.cloned.1.call-update) | async-done | bytes 147472 | tf_op jit(solution)/shard_map/reduce_scatter | solution.py:132
  459.9 1.7 add_convert_fusion
  (17 shorter events, 0.1 us)
Async XLA Ops:
  6.5 326.1 %copy-start = (bf16[1,720,2304]{2,1,0:T(8,128)(2,1)S(1)}, bf16[1,720,2304]{2,1,0:T(8,128)(2,1)}, u32[]{:S(2)}) copy-start(bf16[1,720,2304]{2,1,0:T(8,128)(2,1)} %param.29) | copy-start | bytes 9953284
  6.5 88.4 %all-gather.7.cloned.1.call-start = ((), (), s32[]{:S(2)}) async-start(), calls=%async_computation.5 | async-start | bytes 1216512 | tf_op jit(solution)/shard_map/all_gather | solution.py:64
  9.4 229.8 %all-gather.5.cloned.1.call-start = ((), (), s32[]{:S(2)}) async-start(), calls=%async_computation.4 | async-start | bytes 10616832 | tf_op jit(solution)/shard_map/all_gather | solution.py:86
  17.2 86.2 %copy-start.4 = (bf16[256,288]{0,1:T(8,128)(2,1)S(1)}, bf16[256,288]{0,1:T(8,128)(2,1)}, u32[]{:S(2)}) copy-start(bf16[256,288]{0,1:T(8,128)(2,1)} %param.16) | copy-start | bytes 442372
  140.1 2.4 copy-start.5
  140.1 2.4 copy-start.6
  247.9 3.6 copy-start.1
  247.9 3.6 copy-start.2
  252.6 75.9 %copy-start.7 = (bf16[1,2304,720]{1,2,0:T(8,128)(2,1)S(1)}, bf16[1,2304,720]{1,2,0:T(8,128)(2,1)}, u32[]{:S(2)}) copy-start(bf16[1,2304,720]{1,2,0:T(8,128)(2,1)} %param.27) | copy-start | bytes 9953284
  326.9 1.6 copy-start.3
  347.1 5.8 %copy-start.8 = (bf16[2304,8]{0,1:T(8,128)(2,1)S(1)}, bf16[2304,8]{0,1:T(8,128)(2,1)}, u32[]{:S(2)}) copy-start(bf16[2304,8]{0,1:T(8,128)(2,1)} %param.25) | copy-start | bytes 110596
  347.1 38.1 %all-to-all-start.1 = ((bf16[8,80,2304]{2,1,0:T(8,128)(2,1)}), bf16[8,80,2304]{2,1,0:T(8,128)(2,1)}, u32[]{:S(2)}, u32[]{:S(2)}) async-start(bf16[8,80,2304]{2,1,0:T(8,128)(2,1)} %bitcast.63), calls=%async_computation.1 | async-start | bytes 5898240 | tf_op jit(solution)/shard_map/all_to_all | solution.py:114
  352.8 107.1 %reduce-scatter.2.cloned.1.call-start = ((), (), s32[]{:S(2)}) async-start(), calls=%async_computation.3 | async-start | bytes 1327104 | tf_op jit(solution)/shard_map/reduce_scatter | solution.py:132
Sparse Core Ops, SparseCore 0:
  10.8 84.0 all-gather.6
  140.2 98.8 all-gather.4
  391.8 68.0 reduce-scatter.1
